TPU v7x, 32 devices: a whole 2x2x4 slice. The times are simulated.
32 devices in a mesh: row: 8 (over y, x, core), col: 4 (over z).
Axes of the slice: x: 2, y: 2, z: 4, core: 2. Of those that a mesh axis runs over, the one named last changes fastest.
Arguments:
- struct_basis: float32 [8192, 1024], P(('row', 'col')), may hold values from -6 to 6
- fluid_basis: float32 [4096, 1024], P(('row', 'col')), may hold values from -6 to 6
- stiff_tiles: float32 [64, 4, 128, 128], P(('row', 'col')), may hold values from -0.0029296875 to 0.0029296875
- mass_tiles: float32 [64, 4, 128, 128], P(('row', 'col')), may hold values from -0.0029296875 to 0.0029296875
- fluid_stiff_tiles: float32 [32, 4, 128, 128], P(('row', 'col')), may hold values from -0.00390625 to 0.00390625
- fluid_mass_tiles: float32 [32, 4, 128, 128], P(('row', 'col')), may hold values from -0.00390625 to 0.00390625
- struct_cols: int32 [64, 4], P(('row', 'col')), may hold values from 0 to 3
- fluid_cols: int32 [32, 4], P(('row', 'col')), may hold values from 0 to 2
- wet_rows: int32 [1024], P(('row', 'col')), may hold values from 0 to 127
- wet_dest: int32 [1024, 1], P(('row', 'col')), may hold values from 0 to 31; in each aligned block of 32 rows (0 to 31, 32 to 63, ...) at most 2 rows name the same one
- coupling: float32 [8192, 64], P(('row', 'col')), may hold values from -0.0078125 to 0.0078125
Outputs:
- stiff_red: float32 [1024, 1024], P('row', 'col')
- mass_red: float32 [1024, 1024], P('row', 'col')
- fluid_stiff_red: float32 [1024, 1024], P('row', 'col')
- fluid_mass_red: float32 [1024, 1024], P('row', 'col')
- coupling_red: float32 [1024, 1024], P('row', 'col')
Inputs may be any that keep to these rules, and one draw needn't show every extreme that they name: `wet_dest`: among the 32 entries of one block, no block number is named more than 2 times, and some block number is named exactly 2 times in every draw.
All inputs are finite; a program needn't handle non-finite values.
Results may differ from a plain program's by a relative error of at most 0.0003.
Values sent between devices are 32-bit elements; how exact they have to be, the bound alone decides.
A program may use at most 128 MiB of HBM per device.

v0:
```python
import jax
import jax.numpy as jnp
from jax import lax
from jax.sharding import PartitionSpec as P

R = 1024
TILE = 128
HALO = 1
CAP = 2


exact_precision = lax.Precision.HIGHEST


def from_behind(value, axis, by):
    size = lax.axis_size(axis)
    pairs = [(i, i + by) for i in range(size) if 0 <= i + by < size]
    return lax.ppermute(value, axis, pairs)


def tile_product(tiles, columns, extended):
    blocks = extended.reshape(-1, TILE, R)
    picked = jnp.take(blocks, columns, axis=0)
    result = jnp.einsum("tbij,tbjr->tir", tiles, picked, precision=exact_precision)
    return result.reshape(-1, R)


def congruence(left_basis, image):
    return jnp.einsum("nr,ns->rs", left_basis, image, precision=exact_precision)


def on_device(
    struct_basis,
    fluid_basis,
    stiff_tiles,
    mass_tiles,
    fluid_stiff_tiles,
    fluid_mass_tiles,
    struct_cols,
    fluid_cols,
    wet_rows,
    wet_dest,
    coupling,
):
    border = HALO * TILE
    below_struct, below_fluid = from_behind(
        (struct_basis[-border:], fluid_basis), ("row", "col"), 1
    )
    above_struct, above_fluid = from_behind(
        (struct_basis[:border], fluid_basis), ("row", "col"), -1
    )
    row_count = lax.axis_size("row")
    col_count = lax.axis_size("col")
    shard_count = row_count * col_count
    destination = wet_dest[:, 0]
    onehot = (destination[:, None] == jnp.arange(shard_count, dtype=jnp.int32)[None, :]).astype(
        jnp.int32
    )
    before = jnp.cumsum(onehot, axis=0) - onehot
    slot_index = jnp.sum(before * onehot, axis=1)
    target = destination * CAP + slot_index
    chosen = jnp.take(fluid_basis, wet_rows, axis=0)
    selector = (jnp.arange(shard_count * CAP, dtype=jnp.int32)[:, None] == target[None, :]).astype(
        jnp.float32
    )
    outgoing = jnp.dot(selector, chosen, precision=exact_precision)
    received = lax.all_to_all(outgoing, ("row", "col"), split_axis=0, concat_axis=0, tiled=True)
    extended_struct = jnp.concatenate([below_struct, struct_basis, above_struct], axis=0)
    extended_fluid = jnp.concatenate([below_fluid, fluid_basis, above_fluid], axis=0)
    stiff_part = congruence(struct_basis, tile_product(stiff_tiles, struct_cols, extended_struct))
    mass_part = congruence(struct_basis, tile_product(mass_tiles, struct_cols, extended_struct))
    fstiff_part = congruence(
        fluid_basis, tile_product(fluid_stiff_tiles, fluid_cols, extended_fluid)
    )
    fmass_part = congruence(fluid_basis, tile_product(fluid_mass_tiles, fluid_cols, extended_fluid))
    projected = jnp.einsum("nr,nk->rk", struct_basis, coupling, precision=exact_precision)
    coupled_part = jnp.dot(projected, received, precision=exact_precision)
    first_a, first_b, first_c, first_d, first_e = (
        lax.psum_scatter(stiff_part, "row", scatter_dimension=0, tiled=True),
        lax.psum_scatter(mass_part, "row", scatter_dimension=0, tiled=True),
        lax.psum_scatter(fstiff_part, "row", scatter_dimension=0, tiled=True),
        lax.psum_scatter(fmass_part, "row", scatter_dimension=0, tiled=True),
        lax.psum_scatter(coupled_part, "row", scatter_dimension=0, tiled=True),
    )
    results = (
        lax.psum_scatter(first_a, "col", scatter_dimension=1, tiled=True),
        lax.psum_scatter(first_b, "col", scatter_dimension=1, tiled=True),
        lax.psum_scatter(first_c, "col", scatter_dimension=1, tiled=True),
        lax.psum_scatter(first_d, "col", scatter_dimension=1, tiled=True),
        lax.psum_scatter(first_e, "col", scatter_dimension=1, tiled=True),
    )
    return (results[0], results[1], results[2], results[3], results[4])


def solution(mesh):
    placed = (
        P(("row", "col"), None),
        P(("row", "col"), None),
        P(("row", "col"), None, None, None),
        P(("row", "col"), None, None, None),
        P(("row", "col"), None, None, None),
        P(("row", "col"), None, None, None),
        P(("row", "col"), None),
        P(("row", "col"), None),
        P(("row", "col")),
        P(("row", "col"), None),
        P(("row", "col"), None),
    )
    return jax.shard_map(
        on_device,
        mesh=mesh,
        in_specs=placed,
        out_specs=(
            P("row", "col"),
            P("row", "col"),
            P("row", "col"),
            P("row", "col"),
            P("row", "col"),
        ),
        check_vma=False,
    )
```

profile of v0, /device:TPU:0, one launch (start us, length us, event | category | flops | bytes accessed | tf_op | source)
XLA Modules:
  0.0 448.0 jit_solution(5353736550501227140)
XLA Ops:
  8.6 5.0 %collective-permute-start = (f32[128,1024]{1,0:T(8,128)S(1)}, f32[128,1024]{1,0:T(8,128)S(1)}, u32[]{:S(2)}, u32[]{:S(2)}) collective-permute-start(f32[128,1024]{1,0:T(8,128)S(1)} %get-tuple-element.12), channel_id=1, source_target_pairs={{0,1},{1,2},{2,3},{3,4},{4,5},{5,6},{6,7},{7,8},{8,9},{9,10},{10,1... | collective-permute-start | bytes 1572872 | tf_op jit(solution)/shard_map/ppermute | solution.py:18
  15.0 10.8 %collective-permute-done = f32[128,1024]{1,0:T(8,128)S(1)} collective-permute-done((f32[128,1024]{1,0:T(8,128)S(1)}, f32[128,1024]{1,0:T(8,128)S(1)}, u32[]{:S(2)}, u32[]{:S(2)}) %collective-permute-start) | collective-permute-done | bytes 524320 | tf_op jit(solution)/shard_map/ppermute | solution.py:18
  25.9 13.8 %collective-permute-done.1 = f32[128,1024]{1,0:T(8,128)} collective-permute-done((f32[128,1024]{1,0:T(8,128)S(1)}, f32[128,1024]{1,0:T(8,128)}, u32[]{:S(2)}, u32[]{:S(2)}) %collective-permute-start.1) | collective-permute-done | bytes 524320 | tf_op jit(solution)/shard_map/ppermute | solution.py:18
  46.6 4.5 %fusion = f32[2,1024,128,1]{1,2,3,0:T(8,128)S(1)} fusion(f32[2,4,128,128]{3,2,1,0:T(8,128)S(1)} %copy-done, f32[2,4,128,1024]{3,2,1,0:T(8,128)} %bitcast.74, pred[2,4]{1,0:T(4,128)(4,1)S(1)} %compare_and_fusion), kind=kOutput, calls=%fused_computation.3 | convolution fusion | flops 1611661312 | bytes 5767176 | tf_op jit(solution)/shard_map/tbij,tbjr->tir/dot_general | solution.py:24
  51.1 5.1 %convolution_bitcast_fusion.2 = f32[1024,1024]{0,1:T(8,128)} fusion(f32[256,1024]{1,0:T(8,128)S(1)} %bitcast.79, f32[256,1024]{1,0:T(8,128)S(1)} %copy-done.1), kind=kOutput, calls=%fused_computation.9 | convolution fusion | flops 3221225472 | bytes 6291456 | tf_op jit(solution)/shard_map/nr,ns->rs/dot_general | solution.py:29
  57.3 4.5 %fusion.2 = f32[2,1024,128,1]{1,2,3,0:T(8,128)S(1)} fusion(f32[2,4,128,128]{3,2,1,0:T(8,128)S(1)} %copy-done.3, f32[2,4,128,1024]{3,2,1,0:T(8,128)} %bitcast.75, pred[2,4]{1,0:T(4,128)(4,1)S(1)} %compare_and_fusion), kind=kOutput, calls=%fused_computation.5 | convolution fusion | flops 1611661312 | bytes 5767176 | tf_op jit(solution)/shard_map/tbij,tbjr->tir/dot_general | solution.py:24
  61.8 5.1 %convolution_bitcast_fusion.3 = f32[1024,1024]{0,1:T(8,128)} fusion(f32[256,1024]{1,0:T(8,128)S(1)} %bitcast.78, f32[256,1024]{1,0:T(8,128)S(1)} %copy-done.1), kind=kOutput, calls=%fused_computation.10 | convolution fusion | flops 3221225472 | bytes 6291456 | tf_op jit(solution)/shard_map/nr,ns->rs/dot_general | solution.py:29
  69.3 4.8 %collective-permute-start.2 = (f32[128,1024]{1,0:T(8,128)S(1)}, f32[128,1024]{1,0:T(8,128)S(1)}, u32[]{:S(2)}, u32[]{:S(2)}) collective-permute-start(f32[128,1024]{1,0:T(8,128)S(1)} %copy-done.2), channel_id=1, source_target_pairs={{0,1},{1,2},{2,3},{3,4},{4,5},{5,6},{6,7},{7,8},{8,9},{9,10},{10,1... | collective-permute-start | bytes 1572872 | tf_op jit(solution)/shard_map/ppermute | solution.py:18
  74.1 20.9 %collective-permute-done.3 = f32[128,1024]{1,0:T(8,128)S(1)} collective-permute-done((f32[128,1024]{1,0:T(8,128)S(1)}, f32[128,1024]{1,0:T(8,128)S(1)}, u32[]{:S(2)}, u32[]{:S(2)}) %collective-permute-start.3) | collective-permute-done | bytes 524320 | tf_op jit(solution)/shard_map/ppermute | solution.py:18
  99.8 5.4 %fusion.12 = f32[1024,128]{1,0:T(8,128)S(1)} fusion(f32[4,128,1024]{2,1,0:T(8,128)} %gather_fusion.2, pred[4]{0:T(512)(128)(4,1)S(1)} %and_bitcast_fusion, f32[1,4,128,128]{3,2,1,0:T(8,128)S(1)} %copy-done.4), kind=kOutput, calls=%fused_computation.22 | convolution fusion | flops 805830656 | bytes 2883588 | tf_op jit(solution)/shard_map/tbij,tbjr->tir/dot_general | solution.py:24
  105.2 5.0 %convolution_bitcast_fusion.1 = f32[1024,1024]{0,1:T(8,128)} fusion(f32[1024,128]{1,0:T(8,128)S(1)} %fusion.12, f32[128,1024]{1,0:T(8,128)S(1)} %copy-done.2), kind=kOutput, calls=%fused_computation.8 | convolution fusion | flops 1610612736 | bytes 5242880 | tf_op jit(solution)/shard_map/nr,ns->rs/dot_general | solution.py:29
  111.2 5.1 %fusion.15 = f32[1024,128]{1,0:T(8,128)S(1)} fusion(f32[4,128,1024]{2,1,0:T(8,128)} %gather_fusion.2, pred[4]{0:T(512)(128)(4,1)S(1)} %and_bitcast_fusion, f32[1,4,128,128]{3,2,1,0:T(8,128)S(1)} %copy-done.5), kind=kOutput, calls=%fused_computation.23 | convolution fusion | flops 805830656 | bytes 2883588 | tf_op jit(solution)/shard_map/tbij,tbjr->tir/dot_general | solution.py:24
  116.2 5.0 %convolution_bitcast_fusion = f32[1024,1024]{0,1:T(8,128)} fusion(f32[1024,128]{1,0:T(8,128)S(1)} %fusion.15, f32[128,1024]{1,0:T(8,128)S(1)} %copy-done.2), kind=kOutput, calls=%fused_computation.7 | convolution fusion | flops 1610612736 | bytes 5242880 | tf_op jit(solution)/shard_map/nr,ns->rs/dot_general | solution.py:29
  130.0 8.2 %all-to-all-done = f32[32,2,1024]{2,1,0:T(2,128)S(1)} async-done(((f32[32,2,1024]{2,1,0:T(2,128)}), f32[32,2,1024]{2,1,0:T(2,128)S(1)}, u32[]{:S(2)}, u32[]{:S(2)}) %all-to-all-start) | async-done | bytes 262176 | tf_op jit(solution)/shard_map/all_to_all | solution.py:67
  138.5 4.9 %fusion.38 = f32[1024,1024]{1,0:T(8,128)} fusion(f32[1024,64]{1,0:T(8,128)S(1)} %fusion.37, f32[64,1024]{1,0:T(8,128)S(1)} %all_to_all.10), kind=kOutput, calls=%fused_computation.57 | convolution fusion | flops 805306368 | bytes 4718592 | tf_op jit(solution)/shard_map/dot_general | solution.py:77
  144.0 19.9 %reduce-scatter.11.cloned.1.call-done = f32[128,1024]{0,1:T(8,128)} async-done(((f32[1024,1024]{0,1:T(8,128)}), f32[128,1024]{0,1:T(8,128)}) %reduce-scatter.11.cloned.1.call-update) | async-done | bytes 524304 | tf_op jit(solution)/shard_map/reduce_scatter | solution.py:79
  164.0 54.4 %reduce-scatter.19.cloned.1.call-done = f32[128,1024]{0,1:T(8,128)} async-done(((f32[1024,1024]{0,1:T(8,128)}), f32[128,1024]{0,1:T(8,128)}) %reduce-scatter.19.cloned.1.call-update) | async-done | bytes 524304 | tf_op jit(solution)/shard_map/reduce_scatter | solution.py:81
  218.5 54.2 %reduce-scatter.23.cloned.1.call-done = f32[128,1024]{0,1:T(8,128)} async-done(((f32[1024,1024]{0,1:T(8,128)}), f32[128,1024]{0,1:T(8,128)}) %reduce-scatter.23.cloned.1.call-update) | async-done | bytes 524304 | tf_op jit(solution)/shard_map/reduce_scatter | solution.py:82
  272.7 54.3 %reduce-scatter.27.cloned.1.call-done = f32[128,1024]{1,0:T(8,128)} async-done(((f32[1024,1024]{1,0:T(8,128)}), f32[128,1024]{1,0:T(8,128)}) %reduce-scatter.27.cloned.1.call-update) | async-done | bytes 524304 | tf_op jit(solution)/shard_map/reduce_scatter | solution.py:83
  327.1 24.0 %reduce-scatter.17.cloned.1.call-done = f32[128,256]{0,1:T(8,128)} async-done(((f32[128,1024]{0,1:T(8,128)}), f32[128,256]{0,1:T(8,128)}) %reduce-scatter.17.cloned.1.call-update) | async-done | bytes 131088 | tf_op jit(solution)/shard_map/reduce_scatter | solution.py:87
  352.7 20.7 %reduce-scatter.13.cloned.1.call-done = f32[128,256]{0,1:T(8,128)} async-done(((f32[128,1024]{0,1:T(8,128)}), f32[128,256]{0,1:T(8,128)}) %reduce-scatter.13.cloned.1.call-update) | async-done | bytes 131088 | tf_op jit(solution)/shard_map/reduce_scatter | solution.py:86
  375.1 20.8 %reduce-scatter.21.cloned.1.call-done = f32[128,256]{0,1:T(8,128)} async-done(((f32[128,1024]{0,1:T(8,128)}), f32[128,256]{0,1:T(8,128)}) %reduce-scatter.21.cloned.1.call-update) | async-done | bytes 131088 | tf_op jit(solution)/shard_map/reduce_scatter | solution.py:88
  397.5 20.8 %reduce-scatter.25.cloned.1.call-done = f32[128,256]{0,1:T(8,128)} async-done(((f32[128,1024]{0,1:T(8,128)}), f32[128,256]{0,1:T(8,128)}) %reduce-scatter.25.cloned.1.call-update) | async-done | bytes 131088 | tf_op jit(solution)/shard_map/reduce_scatter | solution.py:89
  420.0 21.2 %reduce-scatter.29.cloned.1.call-done = f32[128,256]{1,0:T(8,128)} async-done(((f32[128,1024]{1,0:T(8,128)}), f32[128,256]{1,0:T(8,128)}) %reduce-scatter.29.cloned.1.call-update) | async-done | bytes 131088 | tf_op jit(solution)/shard_map/reduce_scatter | solution.py:90
  (75 shorter events, 35.2 us)
Async XLA Ops:
  7.2 39.5 %copy-start = (f32[2,4,128,128]{3,2,1,0:T(8,128)S(1)}, f32[2,4,128,128]{3,2,1,0:T(8,128)}, u32[]{:S(2)}) copy-start(f32[2,4,128,128]{3,2,1,0:T(8,128)} %param.18) | copy-start | bytes 1572868
  7.2 32.5 %copy-start.1 = (f32[256,1024]{1,0:T(8,128)S(1)}, f32[256,1024]{1,0:T(8,128)}, u32[]{:S(2)}) copy-start(f32[256,1024]{1,0:T(8,128)} %param.15) | copy-start | bytes 3145732
  7.2 7.7 %copy-start.8 = (s32[2,4]{1,0:T(2,128)S(1)}, s32[2,4]{1,0:T(2,128)}, u32[]{:S(2)}) copy-start(s32[2,4]{1,0:T(2,128)} %param.21) | copy-start | bytes 100
  7.2 136.3 %reduce-scatter.15.cloned.1.call-start = ((), (), s32[]{:S(2)}) async-start(), calls=%async_computation.13 | async-start | bytes 4718592 | tf_op jit(solution)/shard_map/reduce_scatter | solution.py:80
  8.6 17.3 %collective-permute-start = (f32[128,1024]{1,0:T(8,128)S(1)}, f32[128,1024]{1,0:T(8,128)S(1)}, u32[]{:S(2)}, u32[]{:S(2)}) collective-permute-start(f32[128,1024]{1,0:T(8,128)S(1)} %get-tuple-element.12), channel_id=1, source_target_pairs={{0,1},{1,2},{2,3},{3,4},{4,5},{5,6},{6,7},{7,8},{8,9},{9,10},{10,1... | collective-permute-start | bytes 1572872 | tf_op jit(solution)/shard_map/ppermute | solution.py:18
  13.6 26.1 %collective-permute-start.1 = (f32[128,1024]{1,0:T(8,128)S(1)}, f32[128,1024]{1,0:T(8,128)}, u32[]{:S(2)}, u32[]{:S(2)}) collective-permute-start(f32[128,1024]{1,0:T(8,128)S(1)} %get-tuple-element.13), channel_id=1, source_target_pairs={{1,0},{2,1},{3,2},{4,3},{5,4},{6,5},{7,6},{8,7},{9,8},{10,9},{11,1... | collective-permute-start | bytes 1572872 | tf_op jit(solution)/shard_map/ppermute | solution.py:18
  56.2 1.0 copy-start.3
  56.3 107.7 %reduce-scatter.11.cloned.1.call-start = ((), (), s32[]{:S(2)}) async-start(), calls=%async_computation.11 | async-start | bytes 4718592 | tf_op jit(solution)/shard_map/reduce_scatter | solution.py:79
  66.9 1.1 copy-start.2
  66.9 7.1 %copy-start.9 = (s32[1,4]{1,0:T(1,128)S(1)}, s32[1,4]{1,0:T(1,128)}, u32[]{:S(2)}) copy-start(s32[1,4]{1,0:T(1,128)} %param.22) | copy-start | bytes 52
  66.9 151.5 %reduce-scatter.19.cloned.1.call-start = ((), (), s32[]{:S(2)}) async-start(), calls=%async_computation.15 | async-start | bytes 4718592 | tf_op jit(solution)/shard_map/reduce_scatter | solution.py:81
  68.0 27.0 %collective-permute-start.3 = (f32[128,1024]{1,0:T(8,128)S(1)}, f32[128,1024]{1,0:T(8,128)S(1)}, u32[]{:S(2)}, u32[]{:S(2)}) collective-permute-start(f32[128,1024]{1,0:T(8,128)S(1)} %copy-done.2), channel_id=1, source_target_pairs={{1,0},{2,1},{3,2},{4,3},{5,4},{6,5},{7,6},{8,7},{9,8},{10,9},{11,1... | collective-permute-start | bytes 1572872 | tf_op jit(solution)/shard_map/ppermute | solution.py:18
  69.3 25.7 %collective-permute-start.2 = (f32[128,1024]{1,0:T(8,128)S(1)}, f32[128,1024]{1,0:T(8,128)S(1)}, u32[]{:S(2)}, u32[]{:S(2)}) collective-permute-start(f32[128,1024]{1,0:T(8,128)S(1)} %copy-done.2), channel_id=1, source_target_pairs={{0,1},{1,2},{2,3},{3,4},{4,5},{5,6},{6,7},{7,8},{8,9},{9,10},{10,1... | collective-permute-start | bytes 1572872 | tf_op jit(solution)/shard_map/ppermute | solution.py:18
  96.3 3.5 copy-start.4
  110.2 162.4 %reduce-scatter.23.cloned.1.call-start = ((), (), s32[]{:S(2)}) async-start(), calls=%async_computation.17 | async-start | bytes 4718592 | tf_op jit(solution)/shard_map/reduce_scatter | solution.py:82
  121.2 1.3 copy-start.7
  121.9 6.3 %copy-start.6 = (f32[256,64]{0,1:T(8,128)S(1)}, f32[256,64]{0,1:T(8,128)}, u32[]{:S(2)}) copy-start(f32[256,64]{0,1:T(8,128)} %param.25) | copy-start | bytes 196612
  124.1 14.2 %all-to-all-start = ((f32[32,2,1024]{2,1,0:T(2,128)}), f32[32,2,1024]{2,1,0:T(2,128)S(1)}, u32[]{:S(2)}, u32[]{:S(2)}) async-start(f32[32,2,1024]{2,1,0:T(2,128)} %all_to_all.8), calls=%async_computation.8 | async-start | bytes 524288 | tf_op jit(solution)/shard_map/all_to_all | solution.py:67
  127.9 199.1 %reduce-scatter.27.cloned.1.call-start = ((), (), s32[]{:S(2)}) async-start(), calls=%async_computation.19 | async-start | bytes 4718592 | tf_op jit(solution)/shard_map/reduce_scatter | solution.py:83
  143.4 207.7 %reduce-scatter.17.cloned.1.call-start = ((), (), s32[]{:S(2)}) async-start(), calls=%async_computation.14 | async-start | bytes 655360 | tf_op jit(solution)/shard_map/reduce_scatter | solution.py:87
  144.0 229.5 %reduce-scatter.13.cloned.1.call-start = ((), (), s32[]{:S(2)}) async-start(), calls=%async_computation.12 | async-start | bytes 655360 | tf_op jit(solution)/shard_map/reduce_scatter | solution.py:86
  164.0 231.9 %reduce-scatter.21.cloned.1.call-start = ((), (), s32[]{:S(2)}) async-start(), calls=%async_computation.16 | async-start | bytes 655360 | tf_op jit(solution)/shard_map/reduce_scatter | solution.py:88
  218.4 199.9 %reduce-scatter.25.cloned.1.call-start = ((), (), s32[]{:S(2)}) async-start(), calls=%async_computation.18 | async-start | bytes 655360 | tf_op jit(solution)/shard_map/reduce_scatter | solution.py:89
  272.7 168.5 %reduce-scatter.29.cloned.1.call-start = ((), (), s32[]{:S(2)}) async-start(), calls=%async_computation.20 | async-start | bytes 655360 | tf_op jit(solution)/shard_map/reduce_scatter | solution.py:90
  (2 other events, 1.6 us)
Sparse Core Ops, SparseCore 0:
  56.4 53.0 reduce-scatter.14
  112.9 51.0 reduce-scatter.10
  167.3 51.0 reduce-scatter.18
  221.6 51.0 reduce-scatter.22
  275.9 51.1 reduce-scatter.26
  329.2 21.8 reduce-scatter.16
  353.3 20.0 reduce-scatter.12
  375.7 20.1 reduce-scatter.20
  398.2 20.1 reduce-scatter.24
  421.0 20.1 reduce-scatter.28
where the time goes:
time: 449 us; the launch traced here: 448 us
  waiting for transfers between devices  345 us (77%)
  matrix products  46.7 us (10%)
  local copies, waits for them, and re-layouts  21.1 us (5%)
  starting transfers between devices  16.8 us (4%)
  between operations  14.4 us (3%)
    reduce_scatter x1, waiting for transfers between devices, on_device(): lax.psum_scatter(fstiff_part, 'row', scatter_dimension=0, tiled=True)  54.4 us
    reduce_scatter x1, waiting for transfers between devices, on_device(): lax.psum_scatter(coupled_part, 'row', scatter_dimension=0, tiled=True)  54.3 us
    reduce_scatter x1, waiting for transfers between devices, on_device(): lax.psum_scatter(fmass_part, 'row', scatter_dimension=0, tiled=True)  54.2 us
    ppermute x4, waiting for transfers between devices, from_behind(): return lax.ppermute(value, axis, pairs)  45.6 us
    reduce_scatter x1, waiting for transfers between devices, on_device(): lax.psum_scatter(first_b, 'col', scatter_dimension=1, tiled=True)  24 us
    reduce_scatter x1, waiting for transfers between devices, on_device(): lax.psum_scatter(first_e, 'col', scatter_dimension=1, tiled=True)  21.2 us
    reduce_scatter x1, waiting for transfers between devices, on_device(): lax.psum_scatter(first_d, 'col', scatter_dimension=1, tiled=True)  20.8 us
    reduce_scatter x1, waiting for transfers between devices, on_device(): lax.psum_scatter(first_c, 'col', scatter_dimension=1, tiled=True)  20.8 us
  transfers between devices with their start and end apart: 15, of which 13 were waited for; matrix products, arithmetic and copies ran while one was open for 11% of the time, Pallas kernels for 0%

commit v1 on v0

v1 whole, which is shorter than its diff:
```python
import functools

import jax
import jax.numpy as jnp
from jax import lax
from jax.experimental import pallas as pl
from jax.experimental.pallas import tpu as pltpu
from jax.sharding import PartitionSpec as P

TILE = 128
HALO = 1
CAP = 2
MATS = 5
VMEM_LIMIT = 67043328
MESH = pl.DeviceIdType.MESH

exact_precision = lax.Precision.HIGHEST


def halves(value):
    high = value.astype(jnp.bfloat16)
    low = (value - high.astype(jnp.float32)).astype(jnp.bfloat16)
    return high, low


def bits_of(size):
    return size.bit_length() - 1


def subset_offsets(bits):
    offsets = [0]
    for bit in bits:
        offsets = [base + extra for extra in (0, 1 << bit) for base in offsets]
    return offsets


def kernel(
    nr,
    nc,
    struct_cols,
    fluid_cols,
    struct,
    fluid,
    stiff_tiles,
    mass_tiles,
    fstiff_tiles,
    fmass_tiles,
    coupling,
    received,
    *refs,
):
    outs = refs[:MATS]
    acc, halo_s, halo_f, left_s, left_f, tiles_s, tiles_f, ext_s, ext_f, image = refs[MATS : MATS + 10]
    landing = refs[MATS + 10 : -4]
    send_sem, recv_sem, halo_send, halo_recv = refs[-4:]
    rows_s, size = struct.shape
    rows_f = fluid.shape[0]
    bm, bn = size // nr, size // nc
    hb = bm // 2
    border = TILE * HALO
    shards = nr * nc
    row, col = lax.axis_index("row"), lax.axis_index("col")
    block = row * nc + col
    following = lax.rem(block + 1, shards)
    previous = lax.rem(block + shards - 1, shards)
    after = (following // nc, lax.rem(following, nc))
    before = (previous // nc, lax.rem(previous, nc))
    row_bits, col_bits = bits_of(nr), bits_of(nc)
    stages = row_bits + col_bits
    my_row = [lax.rem(row // (1 << b), 2) for b in range(row_bits)]
    my_col = [lax.rem(col // (1 << b), 2) for b in range(col_bits)]
    row_peer = [(row + (1 - 2 * my_row[b]) * (1 << b), col) for b in range(row_bits)]
    col_peer = [(row, col + (1 - 2 * my_col[b]) * (1 << b)) for b in range(col_bits)]

    barrier = pltpu.get_barrier_semaphore()
    greeted = [after, before] + row_peer + col_peer
    for device in greeted:
        pl.semaphore_signal(barrier, inc=1, device_id=device, device_id_type=MESH)
    pl.semaphore_wait(barrier, len(greeted))

    def halo_copy(number, source, target, device):
        return pltpu.make_async_remote_copy(
            src_ref=source,
            dst_ref=target,
            send_sem=halo_send.at[number],
            recv_sem=halo_recv.at[number],
            device_id=device,
            device_id_type=MESH,
        )

    halos = [
        halo_copy(0, struct.at[pl.ds(rows_s - border, border)], halo_s.at[0], after),
        halo_copy(1, struct.at[pl.ds(0, border)], halo_s.at[1], before),
        halo_copy(2, fluid.at[pl.ds(rows_f - border, border)], halo_f.at[0], after),
        halo_copy(3, fluid.at[pl.ds(0, border)], halo_f.at[1], before),
    ]
    for copy in halos:
        copy.start()

    def row_order(half):
        order = list(range(row_bits))
        return order if half == 0 else order[:1] + order[1:][::-1]

    def exchange(half, mat, stage):
        if stage < row_bits:
            order, mine, peers, at = row_order(half), my_row, row_peer, stage
        else:
            order, mine, peers, at = list(range(col_bits)), my_col, col_peer, stage - row_bits
        fixed = sum((mine[b] * (1 << b) for b in order[:at]), 0)
        bit = order[at]
        rest = subset_offsets(order[at + 1 :])
        sent = [fixed + (1 - mine[bit]) * (1 << bit) + extra for extra in rest]
        kept = [fixed + mine[bit] * (1 << bit) + extra for extra in rest]
        return sent, kept, peers[bit]

    def whole_stage(half, mat, stage):
        peer = exchange(half, mat, stage)[2]
        return pltpu.make_async_remote_copy(
            src_ref=landing[stage].at[half, mat],
            dst_ref=landing[stage].at[half, mat],
            send_sem=send_sem.at[half, mat, stage],
            recv_sem=recv_sem.at[half, mat, stage],
            device_id=peer,
            device_id_type=MESH,
        )

    def send(half, mat, stage):
        sent, kept, peer = exchange(half, mat, stage)
        for place, index in enumerate(sent):
            if stage < row_bits:
                source = acc.at[half, mat, index]
            else:
                source = acc.at[half, mat, row, index]
            pltpu.make_async_remote_copy(
                src_ref=source,
                dst_ref=landing[stage].at[half, mat, place],
                send_sem=send_sem.at[half, mat, stage],
                recv_sem=recv_sem.at[half, mat, stage],
                device_id=peer,
                device_id_type=MESH,
            ).start()

    def absorb(half, mat, stage):
        sent, kept, peer = exchange(half, mat, stage)
        whole_stage(half, mat, stage).wait_recv()
        for place, index in enumerate(kept):
            if stage < row_bits:

                def add(c, carry, place=place, index=index):
                    acc[half, mat, index, c] = acc[half, mat, index, c] + landing[stage][half, mat, place, c]
                    return carry

                lax.fori_loop(0, nc, add, 0)
            elif stage < stages - 1:
                acc[half, mat, row, index] = acc[half, mat, row, index] + landing[stage][half, mat, place]
            else:
                outs[mat][pl.ds(half * hb, hb), :] = acc[half, mat, row, index] + landing[stage][half, mat, place]
        if stage < stages - 1:
            send(half, mat, stage + 1)

    def transpose_into(left, source, count):
        def step(k, carry):
            at = pl.ds(pl.multiple_of(k * TILE, TILE), TILE)
            high, low = halves(source[:, at].T)
            left[at, pl.ds(0, count)] = high
            left[at, pl.ds(count, count)] = high
            left[at, pl.ds(2 * count, count)] = low
            return carry

        lax.fori_loop(0, size // TILE, step, 0)

    def columns(c):
        return pl.ds(pl.multiple_of(c * bn, bn), bn)

    def store_image(value, at, count):
        high, low = halves(value)
        image[pl.ds(0, count), at] = high
        image[pl.ds(count, count), at] = low
        image[pl.ds(2 * count, count), at] = high

    def project(left, count, mat):
        def step(c, carry):
            part = jnp.dot(
                left[...], image[pl.ds(0, 3 * count), columns(c)], preferred_element_type=jnp.float32
            )
            for r in range(nr):
                for half in range(2):
                    start = r * bm + half * hb
                    acc[half, mat, r, c] = part[start : start + hb]
            return carry

        lax.fori_loop(0, nc, step, 0)
        for half in range(2):
            send(half, mat, 0)

    def coupled():
        ch, cl = halves(coupling[...])

        def step(c, carry):
            at = columns(c)
            rh, rl = halves(received[:, at])
            value = jnp.dot(ch, rh, preferred_element_type=jnp.float32)
            value += jnp.dot(ch, rl, preferred_element_type=jnp.float32)
            value += jnp.dot(cl, rh, preferred_element_type=jnp.float32)
            store_image(value, at, rows_s)
            return carry

        lax.fori_loop(0, nc, step, 0)
        project(left_s, rows_s, 0)

    def place_rows(ext, total, start, value):
        count = value.shape[0]
        high, low = halves(value)
        ext[pl.ds(start, count), :] = high
        ext[pl.ds(total + start, count), :] = low
        ext[pl.ds(2 * total + start, count), :] = high

    def fill_ext(ext, own, halo, first, second):
        total = own.shape[0] + 2 * border
        place_rows(ext, total, border, own[...])
        halos[first].wait_recv()
        halos[second].wait_recv()
        place_rows(ext, total, 0, jnp.where(block > 0, halo[0], 0.0))
        place_rows(ext, total, total - border, jnp.where(block < shards - 1, halo[1], 0.0))

    def sparse_image(tiles, cols, dense, ext, rows, left, mat):
        total = rows + 2 * border
        for i in range(rows // TILE):
            for c in range(total // TILE):
                tile = jnp.zeros((TILE, TILE), jnp.float32)
                for k in range(tiles.shape[1]):
                    tile += jnp.where(cols[i, k] == c, tiles[i, k], 0.0)
                high, low = halves(tile)
                at = pl.ds(i * TILE, TILE)
                dense[at, pl.ds(c * TILE, TILE)] = high
                dense[at, pl.ds(total + c * TILE, TILE)] = high
                dense[at, pl.ds(2 * total + c * TILE, TILE)] = low

        def step(c, carry):
            at = columns(c)
            store_image(jnp.dot(dense[...], ext[:, at], preferred_element_type=jnp.float32), at, rows)
            return carry

        lax.fori_loop(0, nc, step, 0)
        project(left, rows, mat)

    def compute(mat):
        if mat == 0:
            transpose_into(left_s, struct, rows_s)
            coupled()
        elif mat == 1:
            fill_ext(ext_s, struct, halo_s, 0, 1)
            sparse_image(stiff_tiles, struct_cols, tiles_s, ext_s, rows_s, left_s, 1)
        elif mat == 2:
            sparse_image(mass_tiles, struct_cols, tiles_s, ext_s, rows_s, left_s, 2)
        elif mat == 3:
            transpose_into(left_f, fluid, rows_f)
            fill_ext(ext_f, fluid, halo_f, 2, 3)
            sparse_image(fstiff_tiles, fluid_cols, tiles_f, ext_f, rows_f, left_f, 3)
        else:
            sparse_image(fmass_tiles, fluid_cols, tiles_f, ext_f, rows_f, left_f, 4)

    for step in range(MATS + stages):
        if step < MATS:
            compute(step)
        for stage in range(stages):
            mat = step - 1 - stage
            if 0 <= mat < MATS:
                for half in range(2):
                    absorb(half, mat, stage)

    for copy in halos:
        copy.wait_send()
    for mat in range(MATS):
        for half in range(2):
            for stage in range(stages):
                whole_stage(half, mat, stage).wait_send()


def reduced(nr, nc, struct_cols, fluid_cols, *operands):
    struct, fluid = operands[0], operands[1]
    rows_s, size = struct.shape
    rows_f = fluid.shape[0]
    bm, bn = size // nr, size // nc
    hb = bm // 2
    row_bits, col_bits = bits_of(nr), bits_of(nc)
    stages = row_bits + col_bits
    border = TILE * HALO
    total_s, total_f = rows_s + 2 * border, rows_f + 2 * border
    f32, bf16 = jnp.float32, jnp.bfloat16
    landing = [pltpu.VMEM((2, MATS, nr >> (s + 1), nc, hb, bn), f32) for s in range(row_bits)]
    landing += [pltpu.VMEM((2, MATS, nc >> (s + 1), hb, bn), f32) for s in range(col_bits)]
    smem = pl.BlockSpec(memory_space=pltpu.SMEM)
    vmem = pl.BlockSpec(memory_space=pltpu.VMEM)
    return pl.pallas_call(
        functools.partial(kernel, nr, nc),
        out_shape=[jax.ShapeDtypeStruct((bm, bn), f32)] * MATS,
        in_specs=[smem, smem] + [vmem] * len(operands),
        out_specs=[vmem] * MATS,
        scratch_shapes=[
            pltpu.VMEM((2, MATS, nr, nc, hb, bn), f32),
            pltpu.VMEM((2, border, size), f32),
            pltpu.VMEM((2, border, size), f32),
            pltpu.VMEM((size, 3 * rows_s), bf16),
            pltpu.VMEM((size, 3 * rows_f), bf16),
            pltpu.VMEM((rows_s, 3 * total_s), bf16),
            pltpu.VMEM((rows_f, 3 * total_f), bf16),
            pltpu.VMEM((3 * total_s, size), bf16),
            pltpu.VMEM((3 * total_f, size), bf16),
            pltpu.VMEM((3 * rows_s, size), bf16),
            *landing,
            pltpu.SemaphoreType.DMA((2, MATS, stages)),
            pltpu.SemaphoreType.DMA((2, MATS, stages)),
            pltpu.SemaphoreType.DMA((4,)),
            pltpu.SemaphoreType.DMA((4,)),
        ],
        compiler_params=pltpu.CompilerParams(
            collective_id=0, has_side_effects=True, vmem_limit_bytes=VMEM_LIMIT
        ),
        name="reduced",
    )(struct_cols, fluid_cols, *operands)


def on_device(
    nr,
    nc,
    struct_basis,
    fluid_basis,
    stiff_tiles,
    mass_tiles,
    fluid_stiff_tiles,
    fluid_mass_tiles,
    struct_cols,
    fluid_cols,
    wet_rows,
    wet_dest,
    coupling,
):
    shards = nr * nc
    destination = wet_dest[:, 0]
    same = destination[:, None] == destination[None, :]
    entry = jnp.arange(destination.shape[0], dtype=jnp.int32)
    earlier = entry[None, :] < entry[:, None]
    slot_index = jnp.sum((same & earlier).astype(jnp.int32), axis=1)
    target = destination * CAP + slot_index
    fluid_row = jnp.arange(fluid_basis.shape[0], dtype=jnp.int32)
    slots = jnp.arange(shards * CAP, dtype=jnp.int32)
    hit = (slots[:, None, None] == target[None, None, :]) & (fluid_row[None, :, None] == wet_rows[None, None, :])
    selector = jnp.any(hit, axis=2).astype(jnp.float32)
    outgoing = jnp.dot(selector, fluid_basis, precision=exact_precision)
    received = lax.all_to_all(outgoing, ("row", "col"), split_axis=0, concat_axis=0, tiled=True)
    coupling_red, stiff_red, mass_red, fstiff_red, fmass_red = reduced(
        nr,
        nc,
        struct_cols,
        fluid_cols,
        struct_basis,
        fluid_basis,
        stiff_tiles,
        mass_tiles,
        fluid_stiff_tiles,
        fluid_mass_tiles,
        coupling,
        received,
    )
    return stiff_red, mass_red, fstiff_red, fmass_red, coupling_red


def solution(mesh):
    tiled = P(("row", "col"), None, None, None)
    lined = P(("row", "col"), None)
    return jax.shard_map(
        functools.partial(on_device, mesh.shape["row"], mesh.shape["col"]),
        mesh=mesh,
        in_specs=(lined, lined, tiled, tiled, tiled, tiled, lined, lined, P(("row", "col")), lined, lined),
        out_specs=(P("row", "col"),) * 5,
        check_vma=False,
    )
```

time: 449 us -> 173 us (0.39)
  waiting for transfers between devices: 345 us -> 9.46 us
  Pallas kernels: 0 us -> 144 us
  matrix products: 46.7 us -> 1.36 us
  between operations: 14.4 us -> 0.71 us
  local copies, waits for them, and re-layouts: 21.1 us -> 8.95 us
  starting transfers between devices: 16.8 us -> 7.33 us
    reduce_scatter x10 -> x0, waiting for transfers between devices: 290 us -> none  [the longest x1 54.4 us: on_device(): lax.psum_scatter(fstiff_part, 'row', scatter_dimension=0, tiled=True)]
    pallas_call x0 -> x1, Pallas kernels: none -> 144 us  [reduced(): pl.pallas_call(functools.partial(kernel, nr, nc), out_shape=[jax.ShapeDty...]
    ppermute x4 -> x0, waiting for transfers between devices: 45.6 us -> none  [from_behind(): return lax.ppermute(value, axis, pairs)]
    dot_general x11 -> x1, matrix products: 46.7 us -> 1.36 us  [on_device(): outgoing = jnp.dot(selector, fluid_basis, precision=exact_precision)]
    ppermute x4 -> x0, starting transfers between devices: 12.3 us -> none  [from_behind(): return lax.ppermute(value, axis, pairs)]
    gather x3 -> x0, local copies, waits for them, and re-layouts: 8.49 us -> none  [the longest x2 7.87 us: tile_product(): picked = jnp.take(blocks, columns, axis=0)]
    unnamed x26 -> x20, local copies, waits for them, and re-layouts: 10.1 us -> 7.16 us
  transfers between devices with their start and end apart: 15 -> 1, of which waited for: 13 -> 1; matrix products, arithmetic and copies ran while one was open for 11% -> 0% of each run, Pallas kernels for 0% -> 0%
where the time goes in v1:
time: 173 us; the launch traced here: 172 us
  Pallas kernels  144 us (83%)
  waiting for transfers between devices  9.46 us (5%)
  local copies, waits for them, and re-layouts  8.95 us (5%)
  starting transfers between devices  7.33 us (4%)
    pallas_call x1, Pallas kernels, reduced(): pl.pallas_call(functools.partial(kernel, nr, nc), out_shape=[jax.ShapeDty...  144 us
    all_to_all x1, waiting for transfers between devices, on_device(): lax.all_to_all(outgoing, ('row', 'col'), split_axis=0, concat_axis=0, til...  9.46 us
    all_to_all x1, starting transfers between devices, on_device(): lax.all_to_all(outgoing, ('row', 'col'), split_axis=0, concat_axis=0, til...  7.33 us
    unnamed x20, local copies, waits for them, and re-layouts  7.16 us
  transfers between devices with their start and end apart: 1, of which 1 were waited for; matrix products, arithmetic and copies ran while one was open for 0% of the time, Pallas kernels for 0%

profile of v1, /device:TPU:0, one launch (start us, length us, event | category | flops | bytes accessed | tf_op | source)
XLA Modules:
  0.0 172.1 jit_solution(4867718499908402903)
XLA Ops:
  0.6 0.0 copy-start.6
  0.6 0.6 copy-done.6
  1.3 0.2 convert_reduce_fusion
  1.5 0.6 copy-done.5
  2.1 0.1 iota_compare_fusion.1
  2.2 0.4 and_reduce_fusion
  2.6 1.4 fusion
  4.0 0.9 copy.25
  4.9 7.3 %all-to-all-start = ((f32[32,2,1024]{2,1,0:T(2,128)}), f32[32,2,1024]{2,1,0:T(2,128)S(1)}, u32[]{:S(2)}, u32[]{:S(2)}) async-start(f32[32,2,1024]{2,1,0:T(2,128)} %copy.25), calls=%async_computation | async-start | bytes 524288 | tf_op jit(solution)/shard_map/all_to_all | solution.py:351
  12.2 0.0 copy-done.4
  12.2 0.8 copy.26.coupling
  13.0 9.5 %all-to-all-done = f32[32,2,1024]{2,1,0:T(2,128)S(1)} async-done(((f32[32,2,1024]{2,1,0:T(2,128)}), f32[32,2,1024]{2,1,0:T(2,128)S(1)}, u32[]{:S(2)}, u32[]{:S(2)}) %all-to-all-start) | async-done | bytes 262176 | tf_op jit(solution)/shard_map/all_to_all | solution.py:351
  22.4 0.9 all_to_all.6.received
  23.3 143.6 %reduced.1 = (f32[128,256]{1,0:T(8,128)}, f32[128,256]{1,0:T(8,128)}, f32[128,256]{1,0:T(8,128)}, f32[128,256]{1,0:T(8,128)}, f32[128,256]{1,0:T(8,128)}) custom-call(s32[2,4]{1,0:T(2,128)} %struct_cols.1, s32[1,4]{1,0:T(1,128)} %fluid_cols.1, f32[256,1024]{1,0:T(8,128)} %struct.1, f32[128,1024]{1,0:T(8,128)} %fluid.1, f32[2,4,128,128]{3,2,1,0:T(8,128)} %stiff_tiles.1, ...), custom_call_target="tpu_custom_call" | custom-call | tf_op jit(solution)/shard_map/reduced/pallas_call | solution.py:295
  167.0 0.0 copy-start.3
  167.0 1.6 copy.34
  168.6 0.0 copy-done.3
  168.6 0.7 copy.35
  169.2 0.3 copy-done.2
  169.5 0.7 copy.36
  170.2 0.3 copy-done.1
  170.5 0.7 copy.37
  171.1 0.3 copy-done
  171.4 0.7 copy.38
  (8 shorter events, 0.0 us)
Async XLA Ops:
  0.6 0.7 copy-start.6
  1.5 0.7 copy-start.5
  4.9 7.3 %copy-start.4 = (f32[256,64]{0,1:T(8,128)S(1)}, f32[256,64]{0,1:T(8,128)}, u32[]{:S(2)}) copy-start(f32[256,64]{0,1:T(8,128)} %param.21) | copy-start | bytes 196612
  4.9 17.6 %all-to-all-start = ((f32[32,2,1024]{2,1,0:T(2,128)}), f32[32,2,1024]{2,1,0:T(2,128)S(1)}, u32[]{:S(2)}, u32[]{:S(2)}) async-start(f32[32,2,1024]{2,1,0:T(2,128)} %copy.25), calls=%async_computation | async-start | bytes 524288 | tf_op jit(solution)/shard_map/all_to_all | solution.py:351
  167.0 1.6 copy-start.3
  168.6 1.0 copy-start.2
  169.5 1.0 copy-start.1
  170.5 1.0 copy-start

commit v2 on v1

--- a/solution.py
+++ b/solution.py
@@ -11,10 +11,9 @@
 HALO = 1
 CAP = 2
 MATS = 5
+PARTS = 4
 VMEM_LIMIT = 67043328
 MESH = pl.DeviceIdType.MESH
-
-exact_precision = lax.Precision.HIGHEST
 
 
 def halves(value):
@@ -46,17 +45,18 @@
     fstiff_tiles,
     fmass_tiles,
     coupling,
-    received,
+    selector,
     *refs,
 ):
     outs = refs[:MATS]
     acc, halo_s, halo_f, left_s, left_f, tiles_s, tiles_f, ext_s, ext_f, image = refs[MATS : MATS + 10]
-    landing = refs[MATS + 10 : -4]
-    send_sem, recv_sem, halo_send, halo_recv = refs[-4:]
+    wet_out, wet_in, received = refs[MATS + 10 : MATS + 13]
+    landing = refs[MATS + 13 : -6]
+    send_sem, recv_sem, halo_send, halo_recv, wet_send, wet_recv = refs[-6:]
     rows_s, size = struct.shape
     rows_f = fluid.shape[0]
     bm, bn = size // nr, size // nc
-    hb = bm // 2
+    hb = bm // PARTS
     border = TILE * HALO
     shards = nr * nc
     row, col = lax.axis_index("row"), lax.axis_index("col")
@@ -73,10 +73,23 @@
     col_peer = [(row, col + (1 - 2 * my_col[b]) * (1 << b)) for b in range(col_bits)]
 
     barrier = pltpu.get_barrier_semaphore()
-    greeted = [after, before] + row_peer + col_peer
-    for device in greeted:
-        pl.semaphore_signal(barrier, inc=1, device_id=device, device_id_type=MESH)
-    pl.semaphore_wait(barrier, len(greeted))
+
+    def device_at(distance):
+        other = lax.rem(block + distance, shards)
+        return other, (other // nc, lax.rem(other, nc))
+
+    def greet(distance, carry):
+        pl.semaphore_signal(barrier, inc=1, device_id=device_at(distance)[1], device_id_type=MESH)
+        return carry
+
+    lax.fori_loop(1, shards, greet, 0)
+    high_fluid, low_fluid = halves(fluid[...])
+    chooser = selector[...].astype(jnp.bfloat16)
+    outgoing = jnp.dot(chooser, high_fluid, preferred_element_type=jnp.float32)
+    outgoing += jnp.dot(chooser, low_fluid, preferred_element_type=jnp.float32)
+    for shard in range(shards):
+        wet_out[shard] = outgoing[shard * CAP : (shard + 1) * CAP]
+    pl.semaphore_wait(barrier, shards - 1)
 
     def halo_copy(number, source, target, device):
         return pltpu.make_async_remote_copy(
@@ -94,12 +107,35 @@
         halo_copy(2, fluid.at[pl.ds(rows_f - border, border)], halo_f.at[0], after),
         halo_copy(3, fluid.at[pl.ds(0, border)], halo_f.at[1], before),
     ]
+
+    def send_wet(distance, carry):
+        other, device = device_at(distance)
+        pltpu.make_async_remote_copy(
+            src_ref=wet_out.at[other],
+            dst_ref=wet_in.at[block],
+            send_sem=wet_send,
+            recv_sem=wet_recv,
+            device_id=device,
+            device_id_type=MESH,
+        ).start()
+        return carry
+
+    lax.fori_loop(1, shards, send_wet, 0)
     for copy in halos:
         copy.start()
+    wet_in[block] = wet_out[block]
+    wet_all = pltpu.make_async_remote_copy(
+        src_ref=wet_out.at[pl.ds(0, shards - 1)],
+        dst_ref=wet_in.at[pl.ds(0, shards - 1)],
+        send_sem=wet_send,
+        recv_sem=wet_recv,
+        device_id=after,
+        device_id_type=MESH,
+    )
 
     def row_order(half):
         order = list(range(row_bits))
-        return order if half == 0 else order[:1] + order[1:][::-1]
+        return order if half % 2 == 0 else order[:1] + order[1:][::-1]
 
     def exchange(half, mat, stage):
         if stage < row_bits:
@@ -184,17 +220,20 @@
                 left[...], image[pl.ds(0, 3 * count), columns(c)], preferred_element_type=jnp.float32
             )
             for r in range(nr):
-                for half in range(2):
+                for half in range(PARTS):
                     start = r * bm + half * hb
                     acc[half, mat, r, c] = part[start : start + hb]
             return carry
 
         lax.fori_loop(0, nc, step, 0)
-        for half in range(2):
+        for half in range(PARTS):
             send(half, mat, 0)
 
     def coupled():
         ch, cl = halves(coupling[...])
+        wet_all.wait_recv()
+        for shard in range(shards):
+            received[pl.ds(shard * CAP, CAP), :] = wet_in[shard]
 
         def step(c, carry):
             at = columns(c)
@@ -260,19 +299,35 @@
         else:
             sparse_image(fmass_tiles, fluid_cols, tiles_f, ext_f, rows_f, left_f, 4)
 
-    for step in range(MATS + stages):
-        if step < MATS:
-            compute(step)
-        for stage in range(stages):
-            mat = step - 1 - stage
-            if 0 <= mat < MATS:
-                for half in range(2):
-                    absorb(half, mat, stage)
+    def reduce_stage(mat, stage):
+        for half in range(PARTS):
+            absorb(half, mat, stage)
+
+    compute(0)
+    reduce_stage(0, 0)
+    compute(1)
+    compute(2)
+    reduce_stage(1, 0)
+    reduce_stage(0, 1)
+    reduce_stage(2, 0)
+    reduce_stage(0, 2)
+    reduce_stage(1, 1)
+    compute(3)
+    compute(4)
+    reduce_stage(3, 0)
+    reduce_stage(4, 0)
+    done = {0: 3, 1: 2, 2: 1, 3: 1, 4: 1}
+    while any(done[mat] < stages for mat in done):
+        for mat in reversed(range(MATS)):
+            if done[mat] < stages and (mat == 0 or done[mat] < done[mat - 1]):
+                reduce_stage(mat, done[mat])
+                done[mat] += 1
 
     for copy in halos:
         copy.wait_send()
+    wet_all.wait_send()
     for mat in range(MATS):
-        for half in range(2):
+        for half in range(PARTS):
             for stage in range(stages):
                 whole_stage(half, mat, stage).wait_send()
 
@@ -282,14 +337,15 @@
     rows_s, size = struct.shape
     rows_f = fluid.shape[0]
     bm, bn = size // nr, size // nc
-    hb = bm // 2
+    hb = bm // PARTS
     row_bits, col_bits = bits_of(nr), bits_of(nc)
     stages = row_bits + col_bits
+    shards = nr * nc
     border = TILE * HALO
     total_s, total_f = rows_s + 2 * border, rows_f + 2 * border
     f32, bf16 = jnp.float32, jnp.bfloat16
-    landing = [pltpu.VMEM((2, MATS, nr >> (s + 1), nc, hb, bn), f32) for s in range(row_bits)]
-    landing += [pltpu.VMEM((2, MATS, nc >> (s + 1), hb, bn), f32) for s in range(col_bits)]
+    landing = [pltpu.VMEM((PARTS, MATS, nr >> (s + 1), nc, hb, bn), f32) for s in range(row_bits)]
+    landing += [pltpu.VMEM((PARTS, MATS, nc >> (s + 1), hb, bn), f32) for s in range(col_bits)]
     smem = pl.BlockSpec(memory_space=pltpu.SMEM)
     vmem = pl.BlockSpec(memory_space=pltpu.VMEM)
     return pl.pallas_call(
@@ -298,7 +354,7 @@
         in_specs=[smem, smem] + [vmem] * len(operands),
         out_specs=[vmem] * MATS,
         scratch_shapes=[
-            pltpu.VMEM((2, MATS, nr, nc, hb, bn), f32),
+            pltpu.VMEM((PARTS, MATS, nr, nc, hb, bn), f32),
             pltpu.VMEM((2, border, size), f32),
             pltpu.VMEM((2, border, size), f32),
             pltpu.VMEM((size, 3 * rows_s), bf16),
@@ -308,11 +364,16 @@
             pltpu.VMEM((3 * total_s, size), bf16),
             pltpu.VMEM((3 * total_f, size), bf16),
             pltpu.VMEM((3 * rows_s, size), bf16),
+            pltpu.VMEM((shards, CAP, size), f32),
+            pltpu.VMEM((shards, CAP, size), f32),
+            pltpu.VMEM((shards * CAP, size), f32),
             *landing,
-            pltpu.SemaphoreType.DMA((2, MATS, stages)),
-            pltpu.SemaphoreType.DMA((2, MATS, stages)),
+            pltpu.SemaphoreType.DMA((PARTS, MATS, stages)),
+            pltpu.SemaphoreType.DMA((PARTS, MATS, stages)),
             pltpu.SemaphoreType.DMA((4,)),
             pltpu.SemaphoreType.DMA((4,)),
+            pltpu.SemaphoreType.DMA,
+            pltpu.SemaphoreType.DMA,
         ],
         compiler_params=pltpu.CompilerParams(
             collective_id=0, has_side_effects=True, vmem_limit_bytes=VMEM_LIMIT
@@ -347,8 +408,6 @@
     slots = jnp.arange(shards * CAP, dtype=jnp.int32)
     hit = (slots[:, None, None] == target[None, None, :]) & (fluid_row[None, :, None] == wet_rows[None, None, :])
     selector = jnp.any(hit, axis=2).astype(jnp.float32)
-    outgoing = jnp.dot(selector, fluid_basis, precision=exact_precision)
-    received = lax.all_to_all(outgoing, ("row", "col"), split_axis=0, concat_axis=0, tiled=True)
     coupling_red, stiff_red, mass_red, fstiff_red, fmass_red = reduced(
         nr,
         nc,
@@ -361,7 +420,7 @@
         fluid_stiff_tiles,
         fluid_mass_tiles,
         coupling,
-        received,
+        selector,
     )
     return stiff_red, mass_red, fstiff_red, fmass_red, coupling_red
 

time: 173 us -> 158 us (0.913)
  waiting for transfers between devices: 9.46 us -> 0 us
  starting transfers between devices: 7.33 us -> 0 us
  Pallas kernels: 144 us -> 148 us
  local copies, waits for them, and re-layouts: 8.95 us -> 6.51 us
    all_to_all x1 -> x0, waiting for transfers between devices: 9.46 us -> none  [on_device(): lax.all_to_all(outgoing, ('row', 'col'), split_axis=0, concat_axis=0, til...]
    all_to_all x1 -> x0, starting transfers between devices: 7.33 us -> none  [on_device(): lax.all_to_all(outgoing, ('row', 'col'), split_axis=0, concat_axis=0, til...]
    pallas_call x1, Pallas kernels: 144 us -> 148 us  [reduced(): pl.pallas_call(functools.partial(kernel, nr, nc), out_shape=[jax.ShapeDty...]
    unnamed x20 -> x18, local copies, waits for them, and re-layouts: 7.16 us -> 6.51 us
  transfers between devices with their start and end apart: 1 -> 0, of which waited for: 1 -> 0; matrix products, arithmetic and copies ran while one was open for 0% -> 0% of each run, Pallas kernels for 0% -> 0%
where the time goes in v2:
time: 158 us; the launch traced here: 157 us
  Pallas kernels  148 us (94%)
  local copies, waits for them, and re-layouts  6.51 us (4%)
  other arithmetic  1.92 us (1%)
    pallas_call x1, Pallas kernels, reduced(): pl.pallas_call(functools.partial(kernel, nr, nc), out_shape=[jax.ShapeDty...  148 us
    unnamed x18, local copies, waits for them, and re-layouts  6.51 us

profile of v2, /device:TPU:0, one launch (start us, length us, event | category | flops | bytes accessed | tf_op | source)
XLA Modules:
  0.0 157.3 jit_solution(431645382859707222)
XLA Ops:
  0.6 0.0 copy-start.5
  0.6 0.0 copy-start.4
  0.7 0.6 copy-done.5
  1.3 0.2 convert_reduce_fusion
  1.5 0.7 iota_compare_fusion.1
  2.2 0.4 and_reduce_fusion
  2.6 0.6 convert_element_type.7.selector
  3.2 0.0 copy-done.4
  3.2 0.8 copy.17.coupling
  4.0 148.2 %reduced.1 = (f32[128,256]{1,0:T(8,128)}, f32[128,256]{1,0:T(8,128)}, f32[128,256]{1,0:T(8,128)}, f32[128,256]{1,0:T(8,128)}, f32[128,256]{1,0:T(8,128)}) custom-call(s32[2,4]{1,0:T(2,128)} %struct_cols.1, s32[1,4]{1,0:T(1,128)} %fluid_cols.1, f32[256,1024]{1,0:T(8,128)} %struct.1, f32[128,1024]{1,0:T(8,128)} %fluid.1, f32[2,4,128,128]{3,2,1,0:T(8,128)} %stiff_tiles.1, ...), custom_call_target="tpu_custom_call" | custom-call | tf_op jit(solution)/shard_map/reduced/pallas_call | solution.py:351
  152.2 0.0 copy-start.3
  152.2 1.6 %copy.23 = f32[128,256]{1,0:T(8,128)} copy(f32[128,256]{1,0:T(8,128)} %get-tuple-element.20) | data formatting | bytes 262144
  153.8 0.0 copy-done.3
  153.8 0.0 copy-start.2
  153.8 0.7 copy.24
  154.4 0.3 copy-done.2
  154.7 0.0 copy-start.1
  154.7 0.7 copy.25
  155.4 0.3 copy-done.1
  155.7 0.0 copy-start
  155.7 0.7 copy.26
  156.3 0.3 copy-done
  156.6 0.7 copy.27
  (2 shorter events, 0.0 us)
Async XLA Ops:
  0.6 0.7 copy-start.5
  0.6 2.6 %copy-start.4 = (f32[256,64]{0,1:T(8,128)S(1)}, f32[256,64]{0,1:T(8,128)}, u32[]{:S(2)}) copy-start(f32[256,64]{0,1:T(8,128)} %param.21) | copy-start | bytes 196612
  152.2 1.6 %copy-start.3 = (f32[128,256]{1,0:T(8,128)S(1)}, f32[128,256]{1,0:T(8,128)}, u32[]{:S(2)}) copy-start(f32[128,256]{1,0:T(8,128)} %get-tuple-element.21) | copy-start | bytes 393220
  153.8 1.0 copy-start.2
  154.7 1.0 copy-start.1
  155.7 1.0 copy-start

commit v3 on v2

--- a/solution.py
+++ b/solution.py
@@ -12,6 +12,7 @@
 CAP = 2
 MATS = 5
 PARTS = 4
+EARLY = {3: (0,), 4: (0, 1)}
 VMEM_LIMIT = 67043328
 MESH = pl.DeviceIdType.MESH
 
@@ -48,10 +49,10 @@
     selector,
     *refs,
 ):
-    outs = refs[:MATS]
-    acc, halo_s, halo_f, left_s, left_f, tiles_s, tiles_f, ext_s, ext_f, image = refs[MATS : MATS + 10]
-    wet_out, wet_in, received = refs[MATS + 10 : MATS + 13]
-    landing = refs[MATS + 13 : -6]
+    outs = refs[0]
+    acc, halo_s, halo_f, left_s, left_f, tiles_s, tiles_f, ext_s, ext_f, image = refs[1:11]
+    wet_out, wet_in, received = refs[11:14]
+    landing = refs[14:-6]
     send_sem, recv_sem, halo_send, halo_recv, wet_send, wet_recv = refs[-6:]
     rows_s, size = struct.shape
     rows_f = fluid.shape[0]
@@ -121,8 +122,8 @@
         return carry
 
     lax.fori_loop(1, shards, send_wet, 0)
-    for copy in halos:
-        copy.start()
+    halos[0].start()
+    halos[1].start()
     wet_in[block] = wet_out[block]
     wet_all = pltpu.make_async_remote_copy(
         src_ref=wet_out.at[pl.ds(0, shards - 1)],
@@ -133,21 +134,29 @@
         device_id_type=MESH,
     )
 
-    def row_order(half):
-        order = list(range(row_bits))
-        return order if half % 2 == 0 else order[:1] + order[1:][::-1]
+    def order_of(half, mat):
+        rows = [("row", b) for b in range(row_bits)]
+        cols = [("col", b) for b in range(col_bits)]
+        if half % 2:
+            rows = rows[:1] + rows[1:][::-1]
+        if mat in EARLY and half in EARLY[mat]:
+            return rows[:1] + cols[:1] + rows[1:] + cols[1:]
+        return rows + cols
 
     def exchange(half, mat, stage):
-        if stage < row_bits:
-            order, mine, peers, at = row_order(half), my_row, row_peer, stage
-        else:
-            order, mine, peers, at = list(range(col_bits)), my_col, col_peer, stage - row_bits
-        fixed = sum((mine[b] * (1 << b) for b in order[:at]), 0)
-        bit = order[at]
-        rest = subset_offsets(order[at + 1 :])
-        sent = [fixed + (1 - mine[bit]) * (1 << bit) + extra for extra in rest]
-        kept = [fixed + mine[bit] * (1 << bit) + extra for extra in rest]
-        return sent, kept, peers[bit]
+        order = order_of(half, mat)
+        axis, bit = order[stage]
+        mine = {"row": my_row, "col": my_col}
+        places = {}
+        for name in ("row", "col"):
+            fixed = sum((mine[name][b] * (1 << b) for at, b in order[:stage] if at == name), 0)
+            rest = subset_offsets(sorted(b for at, b in order[stage + 1 :] if at == name))
+            places[name] = [fixed + extra for extra in rest]
+        sent, kept = dict(places), dict(places)
+        sent[axis] = [index + (1 - mine[axis][bit]) * (1 << bit) for index in places[axis]]
+        kept[axis] = [index + mine[axis][bit] * (1 << bit) for index in places[axis]]
+        peer = (row_peer if axis == "row" else col_peer)[bit]
+        return sent, kept, peer
 
     def whole_stage(half, mat, stage):
         peer = exchange(half, mat, stage)[2]
@@ -162,35 +171,44 @@
 
     def send(half, mat, stage):
         sent, kept, peer = exchange(half, mat, stage)
-        for place, index in enumerate(sent):
-            if stage < row_bits:
-                source = acc.at[half, mat, index]
+        width = len(sent["col"])
+        for place, r in enumerate(sent["row"]):
+            if width == nc:
+                pairs = [(acc.at[half, mat, r], landing[stage].at[half, mat, pl.ds(place * nc, nc)])]
             else:
-                source = acc.at[half, mat, row, index]
-            pltpu.make_async_remote_copy(
-                src_ref=source,
-                dst_ref=landing[stage].at[half, mat, place],
-                send_sem=send_sem.at[half, mat, stage],
-                recv_sem=recv_sem.at[half, mat, stage],
-                device_id=peer,
-                device_id_type=MESH,
-            ).start()
+                pairs = [
+                    (acc.at[half, mat, r, c], landing[stage].at[half, mat, place * width + at])
+                    for at, c in enumerate(sent["col"])
+                ]
+            for source, target in pairs:
+                pltpu.make_async_remote_copy(
+                    src_ref=source,
+                    dst_ref=target,
+                    send_sem=send_sem.at[half, mat, stage],
+                    recv_sem=recv_sem.at[half, mat, stage],
+                    device_id=peer,
+                    device_id_type=MESH,
+                ).start()
 
     def absorb(half, mat, stage):
         sent, kept, peer = exchange(half, mat, stage)
         whole_stage(half, mat, stage).wait_recv()
-        for place, index in enumerate(kept):
-            if stage < row_bits:
-
-                def add(c, carry, place=place, index=index):
-                    acc[half, mat, index, c] = acc[half, mat, index, c] + landing[stage][half, mat, place, c]
+        width = len(kept["col"])
+        for place, r in enumerate(kept["row"]):
+            if width == nc:
+
+                def add(c, carry, place=place, r=r):
+                    acc[half, mat, r, c] = acc[half, mat, r, c] + landing[stage][half, mat, place * nc + c]
                     return carry
 
                 lax.fori_loop(0, nc, add, 0)
-            elif stage < stages - 1:
-                acc[half, mat, row, index] = acc[half, mat, row, index] + landing[stage][half, mat, place]
             else:
-                outs[mat][pl.ds(half * hb, hb), :] = acc[half, mat, row, index] + landing[stage][half, mat, place]
+                for at, c in enumerate(kept["col"]):
+                    total = acc[half, mat, r, c] + landing[stage][half, mat, place * width + at]
+                    if stage < stages - 1:
+                        acc[half, mat, r, c] = total
+                    else:
+                        outs[mat, pl.ds(half * hb, hb), :] = total
         if stage < stages - 1:
             send(half, mat, stage + 1)
 
@@ -259,6 +277,9 @@
         place_rows(ext, total, border, own[...])
         halos[first].wait_recv()
         halos[second].wait_recv()
+        if first == 0:
+            halos[2].start()
+            halos[3].start()
         place_rows(ext, total, 0, jnp.where(block > 0, halo[0], 0.0))
         place_rows(ext, total, total - border, jnp.where(block < shards - 1, halo[1], 0.0))
 
@@ -306,8 +327,8 @@
     compute(0)
     reduce_stage(0, 0)
     compute(1)
+    reduce_stage(1, 0)
     compute(2)
-    reduce_stage(1, 0)
     reduce_stage(0, 1)
     reduce_stage(2, 0)
     reduce_stage(0, 2)
@@ -344,15 +365,14 @@
     border = TILE * HALO
     total_s, total_f = rows_s + 2 * border, rows_f + 2 * border
     f32, bf16 = jnp.float32, jnp.bfloat16
-    landing = [pltpu.VMEM((PARTS, MATS, nr >> (s + 1), nc, hb, bn), f32) for s in range(row_bits)]
-    landing += [pltpu.VMEM((PARTS, MATS, nc >> (s + 1), hb, bn), f32) for s in range(col_bits)]
+    landing = [pltpu.VMEM((PARTS, MATS, shards >> (s + 1), hb, bn), f32) for s in range(stages)]
     smem = pl.BlockSpec(memory_space=pltpu.SMEM)
     vmem = pl.BlockSpec(memory_space=pltpu.VMEM)
     return pl.pallas_call(
         functools.partial(kernel, nr, nc),
-        out_shape=[jax.ShapeDtypeStruct((bm, bn), f32)] * MATS,
+        out_shape=jax.ShapeDtypeStruct((MATS, bm, bn), f32),
         in_specs=[smem, smem] + [vmem] * len(operands),
-        out_specs=[vmem] * MATS,
+        out_specs=vmem,
         scratch_shapes=[
             pltpu.VMEM((PARTS, MATS, nr, nc, hb, bn), f32),
             pltpu.VMEM((2, border, size), f32),

time: 158 us -> 141 us (0.89)
  Pallas kernels: 148 us -> 135 us
  local copies, waits for them, and re-layouts: 6.51 us -> 3.4 us
    pallas_call x1, Pallas kernels: 148 us -> 135 us  [reduced(): pl.pallas_call(functools.partial(kernel, nr, nc), out_shape=jax.ShapeDtyp...]
    unnamed x18 -> x5, local copies, waits for them, and re-layouts: 6.51 us -> 1.4 us
    another operation x0 -> x1, local copies, waits for them, and re-layouts: none -> 2 us  [on_device(): coupling_red, stiff_red, mass_red, fstiff_red, fmass_red = reduced(nr, nc...]
where the time goes in v3:
time: 141 us
  Pallas kernels  135 us (96%)
  local copies, waits for them, and re-layouts  3.4 us (2%)
  other arithmetic  1.92 us (1%)
    pallas_call x1, Pallas kernels, reduced(): pl.pallas_call(functools.partial(kernel, nr, nc), out_shape=jax.ShapeDtyp...  135 us

profile of v3, /device:TPU:0, one launch (start us, length us, event | category | flops | bytes accessed | tf_op | source)
XLA Modules:
  0.0 140.6 jit_solution(4225120427045374090)
XLA Ops:
  0.6 0.0 copy-start.1
  0.6 0.0 copy-start
  0.7 0.6 copy-done.1
  1.3 0.2 convert_reduce_fusion
  1.5 0.7 iota_compare_fusion.1
  2.2 0.4 and_reduce_fusion
  2.6 0.6 convert_element_type.7.selector
  3.2 0.0 copy-done
  3.2 0.8 copy.17.coupling
  4.0 134.6 %reduced.1 = f32[5,128,256]{2,1,0:T(8,128)} custom-call(s32[2,4]{1,0:T(2,128)} %struct_cols.1, s32[1,4]{1,0:T(1,128)} %fluid_cols.1, f32[256,1024]{1,0:T(8,128)} %struct.1, f32[128,1024]{1,0:T(8,128)} %fluid.1, f32[2,4,128,128]{3,2,1,0:T(8,128)} %stiff_tiles.1, f32[2,4,128,128]{3,2,1,0:T(8,128)} %mass_tiles.1, f32[1,4,128,128]{3,2,1,0:T(8,128)} %fstiff_tiles.1, ...), custom_call_target="tpu_custom_call" | custom-call | tf_op jit(solution)/shard_map/reduced/pallas_call | solution.py:371
  138.6 2.0 %slice_bitcast_fusion = (f32[128,256]{1,0:T(8,128)}, f32[128,256]{1,0:T(8,128)}, f32[128,256]{1,0:T(8,128)}, f32[128,256]{1,0:T(8,128)}, f32[128,256]{1,0:T(8,128)}) fusion(f32[5,128,256]{2,1,0:T(8,128)} %reduced.1), kind=kLoop, calls=%fused_computation.1 | loop fusion | bytes 1310720 | tf_op jit(solution)/shard_map/unstack | solution.py:431
  (2 shorter events, 0.0 us)
Async XLA Ops:
  0.6 0.7 copy-start.1
  0.6 2.6 %copy-start = (f32[256,64]{0,1:T(8,128)S(1)}, f32[256,64]{0,1:T(8,128)}, u32[]{:S(2)}) copy-start(f32[256,64]{0,1:T(8,128)} %param.21) | copy-start | bytes 196612
